TPU v7x, 32 devices: a whole 2x2x4 slice. The times are simulated.
32 devices in a mesh: band: 4 (over y, core), grid: 8 (over z, x).
Axes of the slice: x: 2, y: 2, z: 4, core: 2. Of those that a mesh axis runs over, the one named last changes fastest.
Arguments:
- wave: float32 [128, 64, 64, 128], P('grid', 'band'), may hold values from -1400 to 1400
- direction: float32 [128, 64, 64, 128], P('grid', 'band'), may hold values from -6 to 6
- potential: float32 [64, 64, 128], P('band', 'grid'), may hold values from -50 to 50
- rotation: float32 [384, 128], replicated, may hold values from -0.3125 to 0.3125
Outputs:
- new_block: float32 [128, 64, 64, 128], P(None, 'band', 'grid')
All inputs are finite; a program needn't handle non-finite values.
Results may differ from a plain program's by a relative error of at most 0.00016.
Values sent between devices are 32-bit elements; how exact they have to be, the bound alone decides.
No kernel may reach another device: no remote copies, remote signals or barrier semaphores. Data moves between devices by JAX's collectives and lax.ppermute only.
A program may use at most 704 MiB of HBM per device.

v0:
```python
import jax
import jax.numpy as jnp
from jax import lax
from jax.sharding import PartitionSpec as P

NX = 64
NY = 64
NZ = 128
STENCIL = (
    -5369.0 / 1800.0,
    12.0 / 7.0,
    -15.0 / 56.0,
    10.0 / 189.0,
    -1.0 / 112.0,
    2.0 / 1925.0,
    -1.0 / 16632.0,
)
LATTICE = 51.3


def with_halo(shard, sides, width):
    for axis, dim in sides:
        devices, length = (lax.axis_size(axis), shard.shape[dim])
        up = [(i, (i + 1) % devices) for i in range(devices)]
        down = [(j, i) for i, j in up]
        last = lax.slice_in_dim(shard, length - width, length, axis=dim)
        initial = lax.slice_in_dim(shard, 0, width, axis=dim)
        before = lax.ppermute(last, axis, up)
        after = lax.ppermute(initial, axis, down)
        shard = jnp.concatenate([before, shard, after], axis=dim)
    return shard


def axis_term(field, axis):
    total = STENCIL[0] * field
    for offset in range(1, 7):
        total = total + STENCIL[offset] * (
            jnp.roll(field, offset, axis) + jnp.roll(field, -offset, axis)
        )
    return total


def inner_products(stacked, ncells):
    high = lax.Precision.HIGHEST
    partial_sum = jnp.dot(stacked, stacked.T, precision=high) / ncells
    return lax.psum(partial_sum, ("band", "grid"))


def apply_basis(coefficients, stacked):
    return lax.dot_general(
        coefficients, stacked, (((0,), (0,)), ((), ())), precision=lax.Precision.HIGHEST
    )


def on_device(wave, direction, potential, rotation):
    local_pot = lax.all_gather(potential, "grid", axis=1, tiled=True)
    bands_here, planes, rows_y, depth = wave.shape
    total_x = planes * lax.axis_size("band")
    inverse_x = (total_x / LATTICE) ** 2
    inverse_y = (rows_y / LATTICE) ** 2
    inverse_z = (depth / LATTICE) ** 2
    padded = with_halo(wave, (("band", 1),), 6)
    along_x = STENCIL[0] * wave
    for offset in range(1, 7):
        along_x = along_x + STENCIL[offset] * (
            padded[:, 6 + offset : 6 + offset + planes]
            + padded[:, 6 - offset : 6 - offset + planes]
        )
    second = along_x * inverse_x + axis_term(wave, 2) * inverse_y + axis_term(wave, 3) * inverse_z
    hwave = -0.5 * second + local_pot[None] * wave
    ncells = NX * NY * NZ
    numer = jnp.sum(wave * hwave, axis=(1, 2, 3))
    denom = jnp.sum(wave * wave, axis=(1, 2, 3))
    numer, denom = lax.psum((numer, denom), "band")
    ritz = numer / denom
    resid = hwave - ritz[:, None, None, None] * wave
    rows_w, rows_r, rows_d = (
        lax.all_to_all(wave, "grid", split_axis=2, concat_axis=0, tiled=True),
        lax.all_to_all(resid, "grid", split_axis=2, concat_axis=0, tiled=True),
        lax.all_to_all(direction, "grid", split_axis=2, concat_axis=0, tiled=True),
    )
    total_bands = rows_w.shape[0]
    out_shape = rows_w.shape
    stacked = jnp.concatenate([rows_r, rows_w, rows_d], axis=0).reshape(3 * total_bands, -1)
    gram = inner_products(stacked, ncells)
    factor = jnp.linalg.cholesky(gram)
    solved = jax.scipy.linalg.solve_triangular(factor, rotation, lower=True, trans=1)
    mixed = apply_basis(solved, stacked)
    return mixed.reshape(out_shape)


def solution(mesh):
    return jax.shard_map(
        on_device,
        mesh=mesh,
        in_specs=(
            P("grid", "band", None, None),
            P("grid", "band", None, None),
            P("band", "grid", None),
            P(),
        ),
        out_specs=P(None, "band", "grid", None),
        check_vma=False,
    )
```

profile of v0, /device:TPU:0, one launch (start us, length us, event | category | flops | bytes accessed | tf_op | source)
XLA Modules:
  0.0 1144.8 jit_solution(8752095945358382932)
XLA Ops:
  6.5 14.2 %constant_dynamic-update-slice_fusion = (f32[16,22,64,128]{3,1,0,2:T(8,128)}, f32[16,16,64,128]{3,1,0,2:T(8,128)}) fusion(f32[16,16,64,128]{3,2,1,0:T(8,128)} %param.4), kind=kLoop, calls=%fused_computation.135 | loop fusion | bytes 25165824
  20.7 7.3 all-to-all-start.1
  28.0 6.7 fusion.91
  35.9 8.3 copy.155
  46.0 1.1 fusion.98
  47.0 1.1 fusion.100
  48.2 1.3 fusion.102
  49.5 12.7 %fusion.103 = (f32[16,16,58,128]{3,1,0,2:T(8,128)}, f32[16,16,58,128]{3,1,0,2:T(8,128)}) fusion(f32[16,16,64,128]{3,1,0,2:T(8,128)} %get-tuple-element.30), kind=kLoop, calls=%fused_computation.159 | loop fusion | bytes 30408704 | tf_op jit(solution)/shard_map/jit(_roll_static)/slice | solution.py:38
  62.2 12.8 %fusion.101 = (f32[16,16,59,128]{3,1,0,2:T(8,128)}, f32[16,16,59,128]{3,1,0,2:T(8,128)}) fusion(f32[16,16,64,128]{3,1,0,2:T(8,128)} %get-tuple-element.30), kind=kLoop, calls=%fused_computation.157 | loop fusion | bytes 30932992 | tf_op jit(solution)/shard_map/jit(_roll_static)/slice | solution.py:38
  75.0 13.0 %fusion.99 = (f32[16,16,60,128]{3,1,0,2:T(8,128)}, f32[16,16,60,128]{3,1,0,2:T(8,128)}) fusion(f32[16,16,64,128]{3,1,0,2:T(8,128)} %get-tuple-element.30), kind=kLoop, calls=%fused_computation.155 | loop fusion | bytes 31457280 | tf_op jit(solution)/shard_map/jit(_roll_static)/slice | solution.py:38
  88.0 11.2 fusion.97
  99.2 11.6 %fusion.95 = (f32[16,16,62,128]{3,1,0,2:T(8,128)}, f32[16,16,62,128]{3,1,0,2:T(8,128)}) fusion(f32[16,16,64,128]{3,1,0,2:T(8,128)} %get-tuple-element.30), kind=kLoop, calls=%fused_computation.151 | loop fusion | bytes 32505856 | tf_op jit(solution)/shard_map/jit(_roll_static)/slice | solution.py:38
  110.8 6.3 fusion.93
  117.1 7.3 fusion.104
  124.4 7.4 fusion.105
  131.8 7.3 fusion.106
  139.1 7.3 fusion.107
  146.5 7.4 fusion.108
  153.9 7.4 fusion.109
  161.2 7.4 fusion.110
  168.6 7.7 fusion.111
  176.2 7.3 fusion.112
  183.5 27.6 %all-to-all-done.1 = f32[16,16,64,128]{3,1,0,2:T(8,128)} async-done(((f32[16,16,64,128]{3,1,0,2:T(8,128)}), f32[16,16,64,128]{3,1,0,2:T(8,128)}, u32[]{:S(2)}, u32[]{:S(2)}) %all-to-all-start.1) | async-done | bytes 8388640 | tf_op jit(solution)/shard_map/all_to_all | solution.py:78
  211.1 5.0 all-to-all-start.2
  216.2 203.3 %all_gather.3 = f32[16,64,128]{2,1,0:T(8,128)S(1)} all-gather(f32[16,8,128]{2,1,0:T(8,128)S(1)} %copy-done.6), channel_id=1, replica_groups=mesh['band'=4,'grid'=8] {'grid'}, dimensions={1}, use_global_device_ids=true | all-gather | bytes 589824 | tf_op jit(solution)/shard_map/all_gather | solution.py:56
  419.8 1.6 fusion.92
  421.4 4.3 multiply_reduce_fusion
  425.7 13.0 %fusion.113 = (f32[16,16,64,123]{3,1,0,2:T(8,128)}, f32[16,16,64,123]{3,1,0,2:T(8,128)}) fusion(f32[16,16,64,128]{3,1,0,2:T(8,128)} %get-tuple-element.30), kind=kLoop, calls=%fused_computation.169 | loop fusion | bytes 32243712 | tf_op jit(solution)/shard_map/jit(_roll_static)/slice | solution.py:38
  438.7 7.4 fusion.114
  446.1 7.3 fusion.115
  453.4 5.9 copy.96
  459.3 6.1 copy_dynamic-update-slice_fusion
  465.4 149.9 %multiply_reduce_fusion.1 = (f32[16]{0:T(128)S(1)}, f32[16,16,64,128]{3,1,0,2:T(8,128)}) fusion(f32[16,16,64,128]{3,2,1,0:T(8,128)} %param.4, f32[16,16,64,128]{3,1,0,2:T(8,128)} %get-tuple-element.30, f32[16,64,128]{2,0,1:T(8,128)S(1)} %copy.146, f32[16,16,64,6]{3,1,0,2:T(8,128)} %get-tuple-element.76, f32[16,16,64,122]{3,1,0,2:T(8,128)} %get-tuple-element.78, ...), kind=kLoop, calls=%fused_computation.90 | loop fusion | flops 197132272 | bytes 280494144 | tf_op jit(solution)/shard_map/reduce_sum | solution.py:72
  615.3 5.7 all-reduce.1
  621.0 14.0 %multiply_subtract_fusion = f32[16,16,64,128]{3,1,0,2:T(8,128)} fusion(f32[16,16,64,128]{3,1,0,2:T(8,128)} %get-tuple-element.24, f32[16]{0:T(128)S(1)} %div.17, f32[16,16,64,128]{3,2,1,0:T(8,128)} %param.4), kind=kLoop, calls=%fused_computation.88 | loop fusion | flops 4194304 | bytes 25165888 | tf_op jit(solution)/shard_map/sub | solution.py:76
  635.0 5.0 all-to-all-start
  640.2 9.3 copy.154
  649.5 9.4 copy.157
  658.9 11.6 %copy.179 = f32[16,16,8,8,128]{4,3,1,0,2:T(8,128)} copy(f32[16,16,8,8,128]{4,1,0,3,2:T(8,128)} %bitcast.4) | data formatting | bytes 16777216 | tf_op jit(solution)/shard_map/all_to_all | solution.py:78
  670.5 9.6 concatenate.160
  680.0 11.6 %copy.178 = f32[16,16,8,8,128]{4,3,1,0,2:T(8,128)} copy(f32[16,16,8,8,128]{4,1,0,3,2:T(8,128)} %bitcast.8) | data formatting | bytes 16777216 | tf_op jit(solution)/shard_map/all_to_all | solution.py:80
  691.6 9.5 concatenate.161
  701.1 122.2 %all-to-all-done = f32[16,16,64,128]{3,1,0,2:T(8,128)} async-done(((f32[16,16,64,128]{3,1,0,2:T(8,128)}), f32[16,16,64,128]{3,1,0,2:T(8,128)}, u32[]{:S(2)}, u32[]{:S(2)}) %all-to-all-start) | async-done | bytes 8388640 | tf_op jit(solution)/shard_map/all_to_all | solution.py:79
  823.3 6.1 copy.151
  829.4 45.4 %fusion.61 = f32[384,384]{0,1:T(8,128)} fusion(f32[128,16,8,128]{3,0,2,1:T(8,128)} %bitcast.90, f32[128,16,8,128]{3,0,2,1:T(8,128)} %bitcast.89, f32[128,16,8,128]{3,0,2,1:T(8,128)S(1)} %bitcast.91), kind=kOutput, calls=%fused_computation.98 | convolution fusion | flops 29003759616 | bytes 25755648 | tf_op jit(solution)/shard_map/dot_general | solution.py:45
  874.8 11.6 %copy.180 = f32[16,16,8,8,128]{4,3,1,0,2:T(8,128)} copy(f32[16,16,8,8,128]{4,1,0,3,2:T(8,128)} %bitcast) | data formatting | bytes 16777216 | tf_op jit(solution)/shard_map/all_to_all | solution.py:79
  886.4 9.4 concatenate.159
  895.8 17.3 %maximum_bitcast_fusion = f32[16384,384]{0,1:T(8,128)} fusion(f32[128,16384]{1,0:T(8,128)} %concatenate.161, f32[128,16384]{1,0:T(8,128)} %concatenate.160, f32[128,16384]{1,0:T(8,128)} %concatenate.159), kind=kLoop, calls=%fused_computation.13 | loop fusion | flops 12582912 | bytes 50331648 | tf_op jit(solution)/shard_map/dot_general | solution.py:50
  913.1 24.9 %copy.160 = f32[16384,384]{1,0:T(8,128)} copy(f32[16384,384]{0,1:T(8,128)} %maximum_bitcast_fusion) | data formatting | bytes 50331648 | tf_op jit(solution)/shard_map/dot_general | solution.py:50
  938.0 63.3 %all-reduce.4.cloned.1.call-done = f32[384,384]{0,1:T(8,128)} async-done(((f32[384,384]{0,1:T(8,128)}), f32[384,384]{0,1:T(8,128)}) %all-reduce.4.cloned.1.call-update) | async-done | bytes 589840 | tf_op jit(solution)/shard_map/psum | solution.py:46
  1001.3 1.3 copy.159
  1002.6 1.1 fusion.64
  1003.7 11.7 %cholesky.77 = f32[128,128]{1,0:T(8,128)S(1)} custom-call(f32[128,128]{1,0:T(8,128)S(1)} %cholesky.192), custom_call_target="Cholesky" | custom-call | tf_op jit(solution)/shard_map/jit(cholesky)/cholesky | solution.py:86
  1015.5 9.8 custom-call.23
  1025.9 11.7 %cholesky.162 = f32[128,128]{1,0:T(8,128)S(1)} custom-call(f32[128,128]{1,0:T(8,128)S(1)} %cholesky.196), custom_call_target="Cholesky" | custom-call | tf_op jit(solution)/shard_map/jit(cholesky)/cholesky | solution.py:86
  1037.6 10.0 custom-call.24
  1048.1 11.7 %cholesky.181 = f32[128,128]{1,0:T(8,128)S(1)} custom-call(f32[128,128]{1,0:T(8,128)S(1)} %convolution_subtract_fusion.3), custom_call_target="Cholesky" | custom-call | tf_op jit(solution)/shard_map/jit(cholesky)/cholesky | solution.py:86
  1063.2 5.7 while.1
  1063.8 1.3 bitcast_dynamic-update-slice_fusion.2
  1065.7 1.3 bitcast_dynamic-update-slice_fusion.2
  1067.6 1.3 bitcast_dynamic-update-slice_fusion.2
  1068.9 29.5 %custom-call.25 = f32[3,128,128]{1,2,0:T(8,128)S(1)} custom-call(f32[3,128,128]{2,1,0:T(8,128)S(1)} %get-tuple-element.12), custom_call_target="InvertDiagBlocksLowerTriangular" | custom-call | tf_op jit(solution)/shard_map/jit(_solve_triangular)/triangular_solve | solution.py:87
  1099.7 29.5 %fusion.65 = f32[128,16,8,128]{3,0,2,1:T(8,128)S(1)} fusion(f32[16,8,128,384]{3,2,1,0:T(8,128)} %bitcast.85, f32[128,128]{1,0:T(8,128)S(1)} %fusion.77, f32[128,128]{1,0:T(8,128)S(1)} %fusion.79, f32[128,128]{1,0:T(8,128)S(1)} %fusion.80), kind=kOutput, calls=%fused_computation.104 | convolution fusion | flops 9663774720 | bytes 33751040 | tf_op jit(solution)/shard_map/dot_general | solution.py:50
  1129.2 8.3 copy.162
  (67 shorter events, 9.2 us)
Async XLA Ops:
  20.7 190.4 %all-to-all-start.1 = ((f32[16,16,64,128]{3,1,0,2:T(8,128)}), f32[16,16,64,128]{3,1,0,2:T(8,128)}, u32[]{:S(2)}, u32[]{:S(2)}) async-start(f32[16,16,64,128]{3,1,0,2:T(8,128)} %get-tuple-element.30), calls=%async_computation.1 | async-start | bytes 16777216 | tf_op jit(solution)/shard_map/all_to_all | solution.py:78
  28.0 7.9 copy-start
  34.7 424.6 %collective-permute-start = (f32[16,6,64,128]{3,2,1,0:T(8,128)}, f32[16,6,64,128]{3,2,1,0:T(8,128)}, u32[]{:S(2)}, u32[]{:S(2)}) collective-permute-start(f32[16,6,64,128]{3,2,1,0:T(8,128)} %get-tuple-element.27), channel_id=1, source_target_pairs={{8,0},{16,8},{24,16},{0,24},{9,1},{17,9},{25,17},{1,25},{10,2},{18... | collective-permute-start | bytes 9437192 | tf_op jit(solution)/shard_map/ppermute | solution.py:29
  35.4 8.8 slice-start
  35.4 8.8 slice-start.1
  35.4 417.9 %collective-permute-start.1 = (f32[16,6,64,128]{3,2,1,0:T(8,128)}, f32[16,6,64,128]{3,2,1,0:T(8,128)}, u32[]{:S(2)}, u32[]{:S(2)}) collective-permute-start(f32[16,6,64,128]{3,2,1,0:T(8,128)} %get-tuple-element.28), channel_id=1, source_target_pairs={{0,8},{8,16},{16,24},{24,0},{1,9},{9,17},{17,25},{25,1},{2,10},{10... | collective-permute-start | bytes 9437192 | tf_op jit(solution)/shard_map/ppermute | solution.py:28
  88.0 22.8 %slice-start.2 = ((s8[8388608]{0:T(1024)(128)(4,1)}), s8[4194304]{0:T(1024)(128)(4,1)S(1)}, s32[]{:S(2)}) async-start(s8[8388608]{0:T(1024)(128)(4,1)} %bitcast.81), calls=%async_computation.6 | async-start | bytes 8388608
  99.2 11.6 %slice-start.3 = ((s8[8388608]{0:T(1024)(128)(4,1)}), s8[4194304]{0:T(1024)(128)(4,1)S(1)}, s32[]{:S(2)}) async-start(s8[8388608]{0:T(1024)(128)(4,1)} %bitcast.81), calls=%async_computation.7 | async-start | bytes 8388608
  183.5 32.7 %copy-start.6 = (f32[16,8,128]{2,1,0:T(8,128)S(1)}, f32[16,8,128]{2,1,0:T(8,128)}, u32[]{:S(2)}) copy-start(f32[16,8,128]{2,1,0:T(8,128)} %param.6) | copy-start | bytes 196612
  211.1 423.8 %all-to-all-start.2 = ((f32[16,16,64,128]{3,1,0,2:T(8,128)}), f32[16,16,64,128]{3,1,0,2:T(8,128)}, u32[]{:S(2)}, u32[]{:S(2)}) async-start(f32[16,16,64,128]{3,1,0,2:T(8,128)} %copy.155), calls=%async_computation.2 | async-start | bytes 16777216 | tf_op jit(solution)/shard_map/all_to_all | solution.py:80
  421.4 17.2 %slice-start.4 = ((s8[8388608]{0:T(1024)(128)(4,1)}), s8[4194304]{0:T(1024)(128)(4,1)S(1)}, s32[]{:S(2)}) async-start(s8[8388608]{0:T(1024)(128)(4,1)} %bitcast.83), calls=%async_computation.8 | async-start | bytes 8388608
  425.7 13.0 %slice-start.5 = ((s8[8388608]{0:T(1024)(128)(4,1)}), s8[4194304]{0:T(1024)(128)(4,1)S(1)}, s32[]{:S(2)}) async-start(s8[8388608]{0:T(1024)(128)(4,1)} %bitcast.83), calls=%async_computation.9 | async-start | bytes 8388608
  453.3 12.0 %copy-start.1 = (f32[16,16,6,128]{3,1,0,2:T(8,128)S(1)}, f32[16,16,6,128]{3,1,0,2:T(8,128)}, u32[]{:S(2)}) copy-start(f32[16,16,6,128]{3,1,0,2:T(8,128)} %get-tuple-element.51) | copy-start | bytes 2359300
  453.3 12.0 %copy-start.2 = (f32[16,16,6,128]{3,1,0,2:T(8,128)S(1)}, f32[16,16,6,128]{3,1,0,2:T(8,128)}, u32[]{:S(2)}) copy-start(f32[16,16,6,128]{3,1,0,2:T(8,128)} %get-tuple-element.52) | copy-start | bytes 2359300
  453.3 12.0 %copy-start.3 = (f32[16,16,5,128]{3,1,0,2:T(8,128)S(1)}, f32[16,16,5,128]{3,1,0,2:T(8,128)}, u32[]{:S(2)}) copy-start(f32[16,16,5,128]{3,1,0,2:T(8,128)} %get-tuple-element.47) | copy-start | bytes 1966084
  453.3 12.0 %copy-start.4 = (f32[16,16,5,128]{3,1,0,2:T(8,128)S(1)}, f32[16,16,5,128]{3,1,0,2:T(8,128)}, u32[]{:S(2)}) copy-start(f32[16,16,5,128]{3,1,0,2:T(8,128)} %get-tuple-element.48) | copy-start | bytes 1966084
  635.0 188.4 %all-to-all-start = ((f32[16,16,64,128]{3,1,0,2:T(8,128)}), f32[16,16,64,128]{3,1,0,2:T(8,128)}, u32[]{:S(2)}, u32[]{:S(2)}) async-start(f32[16,16,64,128]{3,1,0,2:T(8,128)} %multiply_subtract_fusion), calls=%async_computation | async-start | bytes 16777216 | tf_op jit(solution)/shard_map/all_to_all | solution.py:79
  640.0 361.3 %all-reduce.4.cloned.1.call-start = ((), (), s32[]{:S(2)}) async-start(), calls=%async_computation.3 | async-start | bytes 1179648 | tf_op jit(solution)/shard_map/psum | solution.py:46
  913.1 185.3 %copy-start.5 = (f32[384,128]{1,0:T(8,128)S(1)}, f32[384,128]{1,0:T(8,128)}, u32[]{:S(2)}) copy-start(f32[384,128]{1,0:T(8,128)} %param.7) | copy-start | bytes 589828
Sparse Core Ops, SparseCore 0:
  875.0 126.2 all-reduce.3
where the time goes:
time: 1150 us; the launch traced here: 1140 us
  local copies, waits for them, and re-layouts  338 us (29%)
  other arithmetic  273 us (24%)
  waiting for transfers between devices  213 us (19%)
  blocking collectives  209 us (18%)
  matrix products  77.2 us (7%)
  starting transfers between devices  18.7 us (2%)
  between operations  16 us (1%)
    all_gather x1, blocking collectives, on_device(): local_pot = lax.all_gather(potential, 'grid', axis=1, tiled=True)  203 us
    slice x24, local copies, waits for them, and re-layouts, axis_term(): jnp.roll(field, offset, axis) + jnp.roll(field, -offset, axis)  169 us
    reduce_sum x1, other arithmetic, on_device(): numer = jnp.sum(wave * hwave, axis=(1, 2, 3))  150 us
    all_to_all x1, waiting for transfers between devices, on_device(): lax.all_to_all(resid, 'grid', split_axis=2, concat_axis=0, tiled=True)  122 us
    psum x1, waiting for transfers between devices, inner_products(): return lax.psum(partial_sum, ('band', 'grid'))  63.3 us
    another operation x10, other arithmetic, on_device(): factor = jnp.linalg.cholesky(gram)  56.4 us
    dot_general x1, matrix products, inner_products(): partial_sum = jnp.dot(stacked, stacked.T, precision=high) / ncells  45.4 us
    dot_general x2, local copies, waits for them, and re-layouts, apply_basis(): lax.dot_general(coefficients, stacked, (((0,), (0,)), ((), ())), precisio...  33.1 us
  transfers between devices with their start and end apart: 6, of which 3 were waited for; matrix products, arithmetic and copies ran while one was open for 43% of the time, Pallas kernels for 0%

commit v1 on v0

--- a/solution.py
+++ b/solution.py
@@ -16,6 +16,18 @@
     -1.0 / 16632.0,
 )
 LATTICE = 51.3
+
+
+def exchange_directly(x, axis, split, join):
+    ways, here = (lax.axis_size(axis), lax.axis_index(axis))
+    width = x.shape[split] // ways
+    turned = jnp.roll(x, -here * width, axis=split)
+    got = [lax.slice_in_dim(turned, 0, width, axis=split)]
+    for far in range(1, ways):
+        sent = lax.slice_in_dim(turned, far * width, (far + 1) * width, axis=split)
+        got.append(lax.ppermute(sent, axis, [(d, (d + far) % ways) for d in range(ways)]))
+    line = jnp.concatenate(got[::-1], axis=join)
+    return jnp.roll(line, (here + 1) * got[0].shape[join], axis=join)
 
 
 def with_halo(shard, sides, width):
@@ -75,7 +87,7 @@
     ritz = numer / denom
     resid = hwave - ritz[:, None, None, None] * wave
     rows_w, rows_r, rows_d = (
-        lax.all_to_all(wave, "grid", split_axis=2, concat_axis=0, tiled=True),
+        exchange_directly(wave, "grid", 2, 0),
         lax.all_to_all(resid, "grid", split_axis=2, concat_axis=0, tiled=True),
         lax.all_to_all(direction, "grid", split_axis=2, concat_axis=0, tiled=True),
     )

time: 1150 us -> 1210 us (1.052)
  blocking collectives: 209 us -> 58.3 us
  starting transfers between devices: 18.7 us -> 140 us
  waiting for transfers between devices: 213 us -> 271 us
  local copies, waits for them, and re-layouts: 338 us -> 358 us
    ppermute x0 -> x7, waiting for transfers between devices: none -> 210 us  [exchange_directly(): lax.ppermute(sent, axis, [(d, (d + far) % ways) for d in range(ways)])]
    all_gather x1, blocking collectives: 203 us -> 52.6 us  [on_device(): local_pot = lax.all_gather(potential, 'grid', axis=1, tiled=True)]
    ppermute x0 -> x7, starting transfers between devices: none -> 125 us  [exchange_directly(): lax.ppermute(sent, axis, [(d, (d + far) % ways) for d in range(ways)])]
    all_to_all x1, waiting for transfers between devices: 122 us -> 0.01 us  [on_device(): lax.all_to_all(resid, 'grid', split_axis=2, concat_axis=0, tiled=True)]
    all_to_all x1 -> x0, waiting for transfers between devices: 27.6 us -> none  [on_device(): lax.all_to_all(wave, 'grid', split_axis=2, concat_axis=0, tiled=True)]
    unnamed x28 -> x30, local copies, waits for them, and re-layouts: 22.5 us -> 48.6 us
    all_to_all x2 -> x0, local copies, waits for them, and re-layouts: 20.9 us -> none  [on_device(): lax.all_to_all(wave, 'grid', split_axis=2, concat_axis=0, tiled=True)]
    dynamic_slice x0 -> x2, local copies, waits for them, and re-layouts: none -> 14 us  [exchange_directly(): return jnp.roll(line, (here + 1) * got[0].shape[join], axis=join)]
  transfers between devices with their start and end apart: 6 -> 12, of which waited for: 3 -> 4; matrix products, arithmetic and copies ran while one was open for 43% -> 43% of each run, Pallas kernels for 0% -> 0%
where the time goes in v1:
time: 1210 us; the launch traced here: 1200 us
  local copies, waits for them, and re-layouts  358 us (30%)
  other arithmetic  279 us (23%)
  waiting for transfers between devices  271 us (22%)
  starting transfers between devices  140 us (12%)
  matrix products  77 us (6%)
  blocking collectives  58.3 us (5%)
  between operations  16 us (1%)
    ppermute x7, waiting for transfers between devices, exchange_directly(): lax.ppermute(sent, axis, [(d, (d + far) % ways) for d in range(ways)])  210 us
    slice x24, local copies, waits for them, and re-layouts, axis_term(): jnp.roll(field, offset, axis) + jnp.roll(field, -offset, axis)  162 us
    reduce_sum x1, other arithmetic, on_device(): numer = jnp.sum(wave * hwave, axis=(1, 2, 3))  148 us
    ppermute x7, starting transfers between devices, exchange_directly(): lax.ppermute(sent, axis, [(d, (d + far) % ways) for d in range(ways)])  125 us
    psum x1, waiting for transfers between devices, inner_products(): return lax.psum(partial_sum, ('band', 'grid'))  61.3 us
    another operation x10, other arithmetic, on_device(): factor = jnp.linalg.cholesky(gram)  56.6 us
    all_gather x1, blocking collectives, on_device(): local_pot = lax.all_gather(potential, 'grid', axis=1, tiled=True)  52.6 us
    unnamed x30, local copies, waits for them, and re-layouts  48.6 us
  transfers between devices with their start and end apart: 12, of which 4 were waited for; matrix products, arithmetic and copies ran while one was open for 43% of the time, Pallas kernels for 0%

profile of v1, /device:TPU:0, one launch (start us, length us, event | category | flops | bytes accessed | tf_op | source)
XLA Modules:
  0.0 1200.0 jit_solution(4154248248084255472)
XLA Ops:
  6.5 6.7 fusion.92
  13.3 2.4 collective-permute-start
  15.7 8.3 copy.158
  24.0 6.0 all-to-all-start.1
  30.0 14.1 %constant_dynamic-update-slice_fusion = (f32[16,22,64,128]{3,1,0,2:T(8,128)}, f32[16,16,64,128]{3,1,0,2:T(8,128)}) fusion(f32[16,16,64,128]{3,2,1,0:T(8,128)} %param.4), kind=kLoop, calls=%fused_computation.139 | loop fusion | bytes 25165824
  44.1 13.0 %fusion.105 = (f32[16,16,64,1]{3,1,0,2:T(8,128)}, f32[16,16,64,1]{3,1,0,2:T(8,128)}) fusion(f32[16,16,64,128]{3,1,0,2:T(8,128)} %get-tuple-element.30), kind=kLoop, calls=%fused_computation.179 | loop fusion | bytes 262144 | tf_op jit(solution)/shard_map/jit(_roll_static)/slice | solution.py:50
  57.1 7.3 fusion.106
  64.4 7.3 fusion.107
  71.8 7.4 fusion.108
  79.2 7.5 fusion.109
  86.6 7.3 fusion.110
  93.9 7.2 fusion.111
  101.2 7.3 fusion.112
  108.4 7.3 fusion.113
  115.7 6.3 fusion.94
  122.0 6.1 fusion.96
  128.1 6.1 fusion.98
  134.2 13.1 %fusion.100 = (f32[16,16,60,128]{3,1,0,2:T(8,128)}, f32[16,16,60,128]{3,1,0,2:T(8,128)}) fusion(f32[16,16,64,128]{3,1,0,2:T(8,128)} %get-tuple-element.30), kind=kLoop, calls=%fused_computation.174 | loop fusion | bytes 31457280 | tf_op jit(solution)/shard_map/jit(_roll_static)/slice | solution.py:50
  147.4 12.9 %fusion.102 = (f32[16,16,59,128]{3,1,0,2:T(8,128)}, f32[16,16,59,128]{3,1,0,2:T(8,128)}) fusion(f32[16,16,64,128]{3,1,0,2:T(8,128)} %get-tuple-element.30), kind=kLoop, calls=%fused_computation.176 | loop fusion | bytes 30932992 | tf_op jit(solution)/shard_map/jit(_roll_static)/slice | solution.py:50
  160.3 12.7 %fusion.104 = (f32[16,16,58,128]{3,1,0,2:T(8,128)}, f32[16,16,58,128]{3,1,0,2:T(8,128)}) fusion(f32[16,16,64,128]{3,1,0,2:T(8,128)} %get-tuple-element.30), kind=kLoop, calls=%fused_computation.178 | loop fusion | bytes 30408704 | tf_op jit(solution)/shard_map/jit(_roll_static)/slice | solution.py:50
  176.2 2.3 fusion.99
  178.5 2.1 fusion.97
  182.5 52.6 %all_gather.3 = f32[16,64,128]{2,1,0:T(8,128)S(1)} all-gather(f32[16,8,128]{2,1,0:T(8,128)S(1)} %copy-done.3), channel_id=1, replica_groups=mesh['band'=4,'grid'=8] {'grid'}, dimensions={1}, use_global_device_ids=true | all-gather | bytes 589824 | tf_op jit(solution)/shard_map/all_gather | solution.py:68
  237.3 4.1 multiply_reduce_fusion
  241.4 7.7 fusion.114
  249.1 7.3 fusion.115
  256.4 7.4 fusion.116
  263.7 5.8 copy.100
  269.5 5.9 copy_dynamic-update-slice_fusion
  275.5 148.0 %multiply_reduce_fusion.1 = (f32[16]{0:T(128)S(1)}, f32[16,16,64,128]{3,1,0,2:T(8,128)}) fusion(f32[16,16,64,128]{3,2,1,0:T(8,128)} %param.4, f32[16,16,64,128]{3,1,0,2:T(8,128)} %get-tuple-element.30, f32[16,64,128]{2,0,1:T(8,128)S(1)} %copy.150, f32[16,16,64,6]{3,1,0,2:T(8,128)} %get-tuple-element.76, f32[16,16,64,122]{3,1,0,2:T(8,128)} %get-tuple-element.78, ...), kind=kLoop, calls=%fused_computation.92 | loop fusion | flops 197132272 | bytes 280494144 | tf_op jit(solution)/shard_map/reduce_sum | solution.py:84
  423.5 5.7 all-reduce.1
  429.1 14.0 %multiply_subtract_fusion = f32[16,16,64,128]{3,1,0,2:T(8,128)} fusion(f32[16,16,64,128]{3,1,0,2:T(8,128)} %get-tuple-element.24, f32[16]{0:T(128)S(1)} %div.17, f32[16,16,64,128]{3,2,1,0:T(8,128)} %param.4), kind=kLoop, calls=%fused_computation.90 | loop fusion | flops 4194304 | bytes 25165888 | tf_op jit(solution)/shard_map/sub | solution.py:88
  443.2 6.3 all-to-all-start
  449.7 13.3 %copy.156 = f32[16,16,64,128]{3,0,2,1:T(8,128)} copy(f32[16,16,64,128]{3,2,1,0:T(8,128)} %param.4) | data formatting | bytes 16777216 | tf_op args[0]
  463.0 8.4 fusion.6
  471.4 5.7 fusion.117
  477.1 4.7 collective-permute-start.2
  482.4 2.9 collective-permute-start.5
  485.3 123.8 %collective-permute-done.2 = f32[16,16,8,128]{3,0,2,1:T(8,128)S(1)} collective-permute-done((f32[16,16,8,128]{3,0,2,1:T(8,128)S(1)}, f32[16,16,8,128]{3,0,2,1:T(8,128)S(1)}, u32[]{:S(2)}, u32[]{:S(2)}) %collective-permute-start.2) | collective-permute-done | bytes 1048608 | tf_op jit(solution)/shard_map/ppermute | solution.py:28
  609.2 22.5 %collective-permute-done.3 = f32[16,16,8,128]{3,0,2,1:T(8,128)S(1)} collective-permute-done((f32[16,16,8,128]{3,0,2,1:T(8,128)S(1)}, f32[16,16,8,128]{3,0,2,1:T(8,128)S(1)}, u32[]{:S(2)}, u32[]{:S(2)}) %collective-permute-start.3) | collective-permute-done | bytes 1048608 | tf_op jit(solution)/shard_map/ppermute | solution.py:28
  631.6 116.7 %collective-permute-start.8 = (f32[16,16,8,128]{3,0,2,1:T(8,128)}, f32[16,16,8,128]{3,0,2,1:T(8,128)}, u32[]{:S(2)}, u32[]{:S(2)}) collective-permute-start(f32[16,16,8,128]{3,0,2,1:T(8,128)} %get-tuple-element.79), channel_id=1, source_target_pairs={{0,1},{1,2},{2,3},{3,4},{4,5},{5,6},{6,7},{7,0},{8,9},{9,10},{10,1... | collective-permute-start | bytes 3145736 | tf_op jit(solution)/shard_map/ppermute | solution.py:28
  748.7 63.7 %collective-permute-done.5 = f32[16,16,8,128]{3,0,2,1:T(8,128)} collective-permute-done((f32[16,16,8,128]{3,0,2,1:T(8,128)}, f32[16,16,8,128]{3,0,2,1:T(8,128)}, u32[]{:S(2)}, u32[]{:S(2)}) %collective-permute-start.5) | collective-permute-done | bytes 1048608 | tf_op jit(solution)/shard_map/ppermute | solution.py:28
  826.5 4.4 constant_dynamic-slice_fusion.1
  830.8 9.6 copy.163
  840.4 9.0 copy.164
  849.4 9.3 copy.160
  858.7 11.6 copy.181
  870.3 9.4 concatenate.173
  879.7 6.1 copy.155
  885.8 45.3 %fusion.62 = f32[384,384]{0,1:T(8,128)} fusion(f32[128,16,8,128]{3,0,2,1:T(8,128)} %bitcast.77, f32[128,16,8,128]{3,0,2,1:T(8,128)} %constant_dynamic-slice_fusion.1, f32[128,16,8,128]{3,0,2,1:T(8,128)S(1)} %bitcast.78), kind=kOutput, calls=%fused_computation.102 | convolution fusion | flops 29003759616 | bytes 25755648 | tf_op jit(solution)/shard_map/dot_general | solution.py:57
  931.2 11.6 copy.182
  942.8 9.5 concatenate.171
  952.3 17.3 %maximum_bitcast_fusion = f32[16384,384]{0,1:T(8,128)} fusion(f32[128,16384]{1,0:T(8,128)} %concatenate.173, f32[128,16384]{1,0:T(8,128)} %copy.164, f32[128,16384]{1,0:T(8,128)} %concatenate.171), kind=kLoop, calls=%fused_computation.13 | loop fusion | flops 12582912 | bytes 50331648 | tf_op jit(solution)/shard_map/dot_general | solution.py:62
  969.6 25.0 %copy.165 = f32[16384,384]{1,0:T(8,128)} copy(f32[16384,384]{0,1:T(8,128)} %maximum_bitcast_fusion) | data formatting | bytes 50331648 | tf_op jit(solution)/shard_map/dot_general | solution.py:62
  994.6 61.3 %all-reduce.4.cloned.1.call-done = f32[384,384]{0,1:T(8,128)} async-done(((f32[384,384]{0,1:T(8,128)}), f32[384,384]{0,1:T(8,128)}) %all-reduce.4.cloned.1.call-update) | async-done | bytes 589840 | tf_op jit(solution)/shard_map/psum | solution.py:58
  1058.3 11.7 cholesky.77
  1070.1 9.8 custom-call.23
  1080.5 11.7 cholesky.162
  1092.3 10.2 custom-call.24
  1102.9 11.7 cholesky.181
  1118.1 6.3 while.1
  1124.5 29.5 %custom-call.25 = f32[3,128,128]{1,2,0:T(8,128)S(1)} custom-call(f32[3,128,128]{2,1,0:T(8,128)S(1)} %get-tuple-element.12), custom_call_target="InvertDiagBlocksLowerTriangular" | custom-call | tf_op jit(solution)/shard_map/jit(_solve_triangular)/triangular_solve | solution.py:99
  1155.3 29.4 %fusion.66 = f32[128,16,8,128]{3,0,2,1:T(8,128)S(1)} fusion(f32[16,8,128,384]{3,2,1,0:T(8,128)} %bitcast.73, f32[128,128]{1,0:T(8,128)S(1)} %fusion.78, f32[128,128]{1,0:T(8,128)S(1)} %fusion.80, f32[128,128]{1,0:T(8,128)S(1)} %fusion.81), kind=kOutput, calls=%fused_computation.108 | convolution fusion | flops 9663774720 | bytes 33751040 | tf_op jit(solution)/shard_map/dot_general | solution.py:62
  1184.7 8.3 copy.167
  (82 shorter events, 35.0 us)
Async XLA Ops:
  6.5 9.2 copy-start.1
  13.3 256.2 %collective-permute-start = (f32[16,6,64,128]{3,2,1,0:T(8,128)}, f32[16,6,64,128]{3,2,1,0:T(8,128)}, u32[]{:S(2)}, u32[]{:S(2)}) collective-permute-start(f32[16,6,64,128]{3,2,1,0:T(8,128)} %get-tuple-element.27), channel_id=1, source_target_pairs={{8,0},{16,8},{24,16},{0,24},{9,1},{17,9},{25,17},{1,25},{10,2},{18... | collective-permute-start | bytes 9437192 | tf_op jit(solution)/shard_map/ppermute | solution.py:41
  15.7 248.0 %collective-permute-start.1 = (f32[16,6,64,128]{3,2,1,0:T(8,128)}, f32[16,6,64,128]{3,2,1,0:T(8,128)}, u32[]{:S(2)}, u32[]{:S(2)}) collective-permute-start(f32[16,6,64,128]{3,2,1,0:T(8,128)} %get-tuple-element.28), channel_id=1, source_target_pairs={{0,8},{8,16},{16,24},{24,0},{1,9},{9,17},{17,25},{25,1},{2,10},{10... | collective-permute-start | bytes 9437192 | tf_op jit(solution)/shard_map/ppermute | solution.py:40
  24.0 419.2 %all-to-all-start.1 = ((f32[16,16,64,128]{3,1,0,2:T(8,128)}), f32[16,16,64,128]{3,1,0,2:T(8,128)}, u32[]{:S(2)}, u32[]{:S(2)}) async-start(f32[16,16,64,128]{3,1,0,2:T(8,128)} %copy.158), calls=%async_computation.1 | async-start | bytes 16777216 | tf_op jit(solution)/shard_map/all_to_all | solution.py:92
  44.1 13.0 %copy-start = (f32[16,16,64,128]{3,1,0,2:T(8,128)S(1)}, f32[16,16,64,128]{3,1,0,2:T(8,128)}, u32[]{:S(2)}) copy-start(f32[16,16,64,128]{3,1,0,2:T(8,128)} %get-tuple-element.30) | copy-start | bytes 25165828
  173.0 9.5 copy-start.3
  174.6 66.8 %slice-start = ((s8[8388608]{0:T(1024)(128)(4,1)}), s8[4194304]{0:T(1024)(128)(4,1)S(1)}, s32[]{:S(2)}) async-start(s8[8388608]{0:T(1024)(128)(4,1)} %bitcast.71), calls=%async_computation.3 | async-start | bytes 8388608
  235.1 6.2 slice-start.1
  443.2 436.5 %all-to-all-start = ((f32[16,16,64,128]{3,1,0,2:T(8,128)}), f32[16,16,64,128]{3,1,0,2:T(8,128)}, u32[]{:S(2)}, u32[]{:S(2)}) async-start(f32[16,16,64,128]{3,1,0,2:T(8,128)} %multiply_subtract_fusion), calls=%async_computation | async-start | bytes 16777216 | tf_op jit(solution)/shard_map/all_to_all | solution.py:91
  449.4 606.4 %all-reduce.4.cloned.1.call-start = ((), (), s32[]{:S(2)}) async-start(), calls=%async_computation.2 | async-start | bytes 1179648 | tf_op jit(solution)/shard_map/psum | solution.py:58
  477.1 132.1 %collective-permute-start.2 = (f32[16,16,8,128]{3,0,2,1:T(8,128)S(1)}, f32[16,16,8,128]{3,0,2,1:T(8,128)S(1)}, u32[]{:S(2)}, u32[]{:S(2)}) collective-permute-start(f32[16,16,8,128]{3,0,2,1:T(8,128)S(1)} %get-tuple-element.85), channel_id=1, source_target_pairs={{0,7},{1,0},{2,1},{3,2},{4,3},{5,4},{6,5},{7,6},{8,15},{9,8},{10,9... | collective-permute-start | bytes 3145736 | tf_op jit(solution)/shard_map/ppermute | solution.py:28
  481.8 149.8 %collective-permute-start.3 = (f32[16,16,8,128]{3,0,2,1:T(8,128)S(1)}, f32[16,16,8,128]{3,0,2,1:T(8,128)S(1)}, u32[]{:S(2)}, u32[]{:S(2)}) collective-permute-start(f32[16,16,8,128]{3,0,2,1:T(8,128)S(1)} %get-tuple-element.84), channel_id=1, source_target_pairs={{0,6},{1,7},{2,0},{3,1},{4,2},{5,3},{6,4},{7,5},{8,14},{9,15},{10,... | collective-permute-start | bytes 3145736 | tf_op jit(solution)/shard_map/ppermute | solution.py:28
  482.4 266.2 %collective-permute-start.4 = (f32[16,16,8,128]{3,0,2,1:T(8,128)}, f32[16,16,8,128]{3,0,2,1:T(8,128)S(1)}, u32[]{:S(2)}, u32[]{:S(2)}) collective-permute-start(f32[16,16,8,128]{3,0,2,1:T(8,128)} %get-tuple-element.83), channel_id=1, source_target_pairs={{0,5},{1,6},{2,7},{3,0},{4,1},{5,2},{6,3},{7,4},{8,13},{9,14},{10,... | collective-permute-start | bytes 3145736 | tf_op jit(solution)/shard_map/ppermute | solution.py:28
  482.4 330.0 %collective-permute-start.5 = (f32[16,16,8,128]{3,0,2,1:T(8,128)}, f32[16,16,8,128]{3,0,2,1:T(8,128)}, u32[]{:S(2)}, u32[]{:S(2)}) collective-permute-start(f32[16,16,8,128]{3,0,2,1:T(8,128)} %get-tuple-element.82), channel_id=1, source_target_pairs={{0,4},{1,5},{2,6},{3,7},{4,0},{5,1},{6,2},{7,3},{8,12},{9,13},{10,... | collective-permute-start | bytes 3145736 | tf_op jit(solution)/shard_map/ppermute | solution.py:28
  485.3 328.5 %collective-permute-start.6 = (f32[16,16,8,128]{3,0,2,1:T(8,128)}, f32[16,16,8,128]{3,0,2,1:T(8,128)}, u32[]{:S(2)}, u32[]{:S(2)}) collective-permute-start(f32[16,16,8,128]{3,0,2,1:T(8,128)} %get-tuple-element.81), channel_id=1, source_target_pairs={{0,3},{1,4},{2,5},{3,6},{4,7},{5,0},{6,1},{7,2},{8,11},{9,12},{10,... | collective-permute-start | bytes 3145736 | tf_op jit(solution)/shard_map/ppermute | solution.py:28
  609.2 206.0 %collective-permute-start.7 = (f32[16,16,8,128]{3,0,2,1:T(8,128)}, f32[16,16,8,128]{3,0,2,1:T(8,128)}, u32[]{:S(2)}, u32[]{:S(2)}) collective-permute-start(f32[16,16,8,128]{3,0,2,1:T(8,128)} %get-tuple-element.80), channel_id=1, source_target_pairs={{0,2},{1,3},{2,4},{3,5},{4,6},{5,7},{6,0},{7,1},{8,10},{9,11},{10,... | collective-permute-start | bytes 3145736 | tf_op jit(solution)/shard_map/ppermute | solution.py:28
  631.6 184.9 %collective-permute-start.8 = (f32[16,16,8,128]{3,0,2,1:T(8,128)}, f32[16,16,8,128]{3,0,2,1:T(8,128)}, u32[]{:S(2)}, u32[]{:S(2)}) collective-permute-start(f32[16,16,8,128]{3,0,2,1:T(8,128)} %get-tuple-element.79), channel_id=1, source_target_pairs={{0,1},{1,2},{2,3},{3,4},{4,5},{5,6},{6,7},{7,0},{8,9},{9,10},{10,1... | collective-permute-start | bytes 3145736 | tf_op jit(solution)/shard_map/ppermute | solution.py:28
  969.6 184.4 %copy-start.2 = (f32[384,128]{1,0:T(8,128)S(1)}, f32[384,128]{1,0:T(8,128)}, u32[]{:S(2)}) copy-start(f32[384,128]{1,0:T(8,128)} %param.7) | copy-start | bytes 589828
Sparse Core Ops, SparseCore 0:
  931.3 124.5 all-reduce.3
